TPU v7x, 512 devices: a whole 4x4x16 slice. The times are simulated.
512 devices in a mesh: filter: 32 (over z_lo, x), space: 16 (over z_hi, y, core).
Axes of the slice: x: 4, y: 4, z: 16 (z_hi: 2, z_lo: 8; z = z_hi * 8 + z_lo), core: 2. Of those that a mesh axis runs over, the one named last changes fastest.
Arguments:
- volume: bfloat16 [1024, 64, 1024], P('filter', 'space'), may hold values from -6 to 6
- mixing: bfloat16 [1024, 1024], P('filter'), may hold values from -0.1875 to 0.1875
- kernel_taps: float32 [1024, 27], P('filter'), may hold values from -1.25 to 1.25
- upstream: bfloat16 [1024, 64, 1024], P('filter', 'space'), may hold values from -6 to 6
Outputs:
- output: bfloat16 [1024, 64, 1024], P('filter', 'space')
- volume_grad: bfloat16 [1024, 64, 1024], P('filter', 'space')
- mixing_grad: float32 [1024, 1024], P('filter', 'space')
- taps_grad: float32 [1024, 27], P('filter')
All inputs are finite; a program needn't handle non-finite values.
Results may differ from a plain program's by a relative error of at most 0.0055.
Values may be sent and summed in bfloat16 or wider, within the bound.
A program may use at most 64 MiB of HBM per device.

v0:
```python
import math
import jax
import jax.numpy as jnp
from jax import lax
from jax.sharding import PartitionSpec as P

WW = 64


def padded_2(array, sides, width):
    for axis, dim in sides:
        size, length = (lax.axis_size(axis), array.shape[dim])
        up = [(i, (i + 1) % size) for i in range(size - 1)]
        down = [(j, i) for i, j in up]
        last = lax.slice_in_dim(array, length - width, length, axis=dim)
        leading = lax.slice_in_dim(array, 0, width, axis=dim)
        before = lax.ppermute(last, axis, up)
        after = lax.ppermute(leading, axis, down)
        array = jnp.concatenate([before, array, after], axis=dim)
    return array


def pad_rows_cols(field):
    return jnp.pad(field, ((0, 0), (0, 0), (1, 1), (1, 1)))


def depth_conv(padded, kernel_taps, flip):
    depth = padded.shape[1] - 2
    height = padded.shape[2] - 2
    breadth = padded.shape[3] - 2
    summed = jnp.zeros((padded.shape[0], depth, height, breadth), jnp.float32)
    for plane_off in range(3):
        for row_off in range(3):
            for col_off in range(3):
                index_tap = plane_off * 9 + row_off * 3 + col_off
                if flip:
                    plane_at, row_at, col_at = (2 - plane_off, 2 - row_off, 2 - col_off)
                else:
                    plane_at, row_at, col_at = (plane_off, row_off, col_off)
                window = padded[
                    :,
                    plane_at : plane_at + depth,
                    row_at : row_at + height,
                    col_at : col_at + breadth,
                ]
                summed = summed + kernel_taps[:, index_tap][:, None, None, None] * window.astype(
                    jnp.float32
                )
    return summed


def tap_grads(grad_field, padded):
    depth = grad_field.shape[1]
    height = grad_field.shape[2]
    breadth = grad_field.shape[3]
    grad_wide = grad_field.astype(jnp.float32)
    columns_list = []
    for plane_off in range(3):
        for row_off in range(3):
            for col_off in range(3):
                window = padded[
                    :,
                    plane_off : plane_off + depth,
                    row_off : row_off + height,
                    col_off : col_off + breadth,
                ]
                columns_list.append(jnp.sum(grad_wide * window.astype(jnp.float32), axis=(1, 2, 3)))
    return jnp.stack(columns_list, axis=1)


def silu_slope(values):
    sig_val = jax.nn.sigmoid(values)
    return sig_val * (1.0 + values * (1.0 - sig_val))


def body(volume, mixing, kernel_taps, upstream):
    channels = volume.shape[0]
    planes = volume.shape[1]
    flat_cells = volume.shape[2]
    row_count = flat_cells // WW
    slab_cells = planes * flat_cells
    space_count = lax.axis_size("space")
    norm_factor = 1.0 / math.sqrt(planes * space_count * flat_cells)
    flat_vol = volume.reshape(channels, slab_cells)
    vol_all = lax.all_gather(flat_vol, "filter", axis=0, tiled=True)
    mixed = jnp.dot(mixing, vol_all, preferred_element_type=jnp.float32).astype(jnp.bfloat16)
    mixed_grid = mixed.reshape(channels, planes, row_count, WW)
    up_grid = upstream.reshape(channels, planes, row_count, WW)
    mixed_rim = padded_2(mixed_grid, (("space", 1),), 1)
    mixed_pad = pad_rows_cols(mixed_rim)
    spatial = depth_conv(mixed_pad, kernel_taps, False)
    grad_own = (up_grid.astype(jnp.float32) * silu_slope(spatial)).astype(jnp.bfloat16)
    grad_wide = padded_2(grad_own, (("space", 1),), 1)
    vol_grid = volume.reshape(channels, planes, row_count, WW).astype(jnp.float32)
    output = (
        (vol_grid + jax.nn.silu(spatial)).astype(jnp.bfloat16).reshape(channels, planes, flat_cells)
    )
    spatial_grad = grad_wide[:, 1:-1]
    mixed_grad = (
        depth_conv(pad_rows_cols(grad_wide), kernel_taps, True)
        .astype(jnp.bfloat16)
        .reshape(channels, slab_cells)
    )
    taps_part = tap_grads(spatial_grad, mixed_pad) * norm_factor
    taps_grad = lax.psum(taps_part, "space")
    weight_cols = lax.all_to_all(mixing, "filter", split_axis=1, concat_axis=0, tiled=True)
    back_sum = lax.dot_general(
        weight_cols,
        lax.all_gather(mixed_grad, "filter", axis=0, tiled=True),
        (((0,), (0,)), ((), ())),
        preferred_element_type=jnp.float32,
    )
    weight_term = (
        lax.dot_general(
            mixed_grad, vol_all, (((1,), (1,)), ((), ())), preferred_element_type=jnp.float32
        )
        * norm_factor
    )
    mixing_grad = lax.psum_scatter(weight_term, "space", scatter_dimension=1, tiled=True)
    volume_grad = (
        (upstream.reshape(channels, slab_cells).astype(jnp.float32) + back_sum)
        .astype(jnp.bfloat16)
        .reshape(channels, planes, flat_cells)
    )
    return (output, volume_grad, mixing_grad, taps_grad)


def solution(mesh):
    in_specs = (
        P("filter", "space", None),
        P("filter", None),
        P("filter", None),
        P("filter", "space", None),
    )
    out_specs = (
        P("filter", "space", None),
        P("filter", "space", None),
        P("filter", "space"),
        P("filter", None),
    )
    return jax.shard_map(body, mesh=mesh, in_specs=in_specs, out_specs=out_specs, check_vma=False)
```

profile of v0, /device:TPU:2, one launch (start us, length us, event | category | flops | bytes accessed | tf_op | source)
XLA Modules:
  0.0 667.5 jit_solution(4207602100597087472)
XLA Ops:
  7.2 0.0 all-gather.3.cloned.1.call-start
  7.2 1.7 copy.16
  9.0 0.0 all-gather.3.cloned.1.call-update
  9.0 0.0 reduce-scatter.4.cloned.1.call-start
  9.0 1.3 reshape.69
  10.3 2.0 slice_reduce_fusion.26
  12.3 240.9 %all-gather.3.cloned.1.call-done = bf16[1024,4096]{1,0:T(8,128)(2,1)} async-done(((bf16[32,4096]{1,0:T(8,128)(2,1)}), bf16[1024,4096]{1,0:T(8,128)(2,1)}) %all-gather.3.cloned.1.call-update) | async-done | bytes 8388624 | tf_op jit(solution)/shard_map/all_gather | solution.py:85
  253.2 4.9 convolution_convert_fusion
  258.1 0.5 reshape.63
  258.7 1.3 collective-permute-start
  260.0 1.3 collective-permute-start.1
  261.3 0.3 slice_reduce_fusion.25
  261.7 2.8 collective-permute-done.1
  264.5 0.8 select_maximum_fusion.2
  265.3 11.5 %fusion.72 = (f32[32]{0:T(128)S(1)}, f32[32]{0:T(128)S(1)}, f32[32]{0:T(128)S(1)}, f32[32]{0:T(128)S(1)}, f32[32]{0:T(128)}, /*index=5*/f32[32]{0:T(128)}, f32[3...) fusion(bf16[32,6,18,66]{3,2,1,0:T(8,128)(2,1)S(1)} %select_maxi, ...), kind=kLoop, calls=%fused_computation.138 | loop fusion | flops 16776640 | bytes 8001152 | tf_op jit(solution)/shard_map/reduce_sum | solution.py:67
  276.8 5.5 collective-permute-start.2
  282.3 1.3 collective-permute-start.3
  283.6 1.9 collective-permute-done.3
  285.5 0.8 select_maximum_fusion
  286.3 5.8 fusion.73
  292.1 0.5 reshape.65
  292.6 0.0 copy-start.12
  292.6 6.1 convolution_multiply_fusion
  298.7 0.0 copy-done.2
  298.7 1.0 copy.14
  299.8 0.0 reduce-scatter.4.cloned.1.call-update
  299.8 0.0 all-gather.5.cloned.1.call-start
  299.8 0.7 all-gather.5.cloned.1.call-update
  300.5 0.2 copy.11
  300.7 0.8 reshape.99
  301.6 12.2 %all-to-all-start = ((bf16[32,2,512]{2,1,0:T(2,128)(2,1)}), bf16[32,2,512]{2,1,0:T(2,128)(2,1)}, u32[]{:S(2)}, u32[]{:S(2)}) async-start(bf16[32,2,512]{2,1,0:T(2,128)(2,1)} %reshape.99), calls=%async_computation | async-start | bytes 131072 | tf_op jit(solution)/shard_map/all_to_all | solution.py:106
  313.8 0.1 convert_element_type.292
  313.9 1.3 reshape.67
  315.2 1.1 copy.17
  316.3 9.2 %all-to-all-done = bf16[32,2,512]{2,1,0:T(2,128)(2,1)} async-done(((bf16[32,2,512]{2,1,0:T(2,128)(2,1)}), bf16[32,2,512]{2,1,0:T(2,128)(2,1)}, u32[]{:S(2)}, u32[]{:S(2)}) %all-to-all-start) | async-done | bytes 65568 | tf_op jit(solution)/shard_map/all_to_all | solution.py:106
  325.5 1.1 reshape.100
  326.6 0.1 copy.12
  326.7 0.9 all_to_all.17
  327.6 3.0 fusion.71
  330.6 2.9 stack.111
  333.5 126.2 %psum.7 = f32[32,27]{0,1:T(8,128)S(1)} all-reduce(f32[32,27]{0,1:T(8,128)S(1)} %broadcast_multiply_fusion), channel_id=1, replica_groups=mesh['filter'=32,'space'=16] {'space'}, use_global_device_ids=true, to_apply=%region_28.29 | all-reduce | flops 864 | bytes 6912 | tf_op jit(solution)/shard_map/psum | solution.py:105
  459.6 0.7 copy.13
  460.3 1.5 add_convert_fusion
  461.8 1.0 reshape.64
  462.8 1.4 copy.15
  464.3 190.9 %all-gather.5.cloned.1.call-done = bf16[1024,4096]{1,0:T(8,128)(2,1)} async-done(((bf16[32,4096]{1,0:T(8,128)(2,1)}), bf16[1024,4096]{1,0:T(8,128)(2,1)}) %all-gather.5.cloned.1.call-update) | async-done | bytes 8388624 | tf_op jit(solution)/shard_map/all_gather | solution.py:109
  655.2 4.9 fusion.1
  660.1 0.9 reshape.66
  (31 shorter events, 0.1 us)
Async XLA Ops:
  7.2 246.1 %copy-start.11 = (bf16[32,1024]{1,0:T(8,128)(2,1)S(1)}, bf16[32,1024]{1,0:T(8,128)(2,1)}, u32[]{:S(2)}) copy-start(bf16[32,1024]{1,0:T(8,128)(2,1)} %param.5) | copy-start | bytes 196612
  7.2 246.0 %all-gather.3.cloned.1.call-start = ((), (), s32[]{:S(2)}) async-start(), calls=%async_computation.2 | async-start | bytes 8650752 | tf_op jit(solution)/shard_map/all_gather | solution.py:85
  9.0 453.8 %reduce-scatter.4.cloned.1.call-start = ((), (), s32[]{:S(2)}) async-start(), calls=%async_computation.4 | async-start | bytes 557056
  12.3 249.0 %copy-start = (f32[32,27]{1,0:T(8,128)S(1)}, f32[32,27]{1,0:T(8,128)}, u32[]{:S(2)}) copy-start(f32[32,27]{1,0:T(8,128)} %param.6) | copy-start | bytes 10372
  258.7 2.9 collective-permute-start
  260.0 4.5 collective-permute-start.1
  261.7 15.1 %copy-start.4 = (bf16[32,1,16,64]{3,2,1,0:T(8,128)(2,1)}, bf16[32,1,16,64]{3,2,1,0:T(8,128)(2,1)S(1)}, u32[]{:S(2)}) copy-start(bf16[32,1,16,64]{3,2,1,0:T(8,128)(2,1)S(1)} %collective-permute-done) | copy-start | bytes 196612
  264.5 12.3 %copy-start.6 = (bf16[32,1,16,64]{3,2,1,0:T(8,128)(2,1)}, bf16[32,1,16,64]{3,2,1,0:T(8,128)(2,1)S(1)}, u32[]{:S(2)}) copy-start(bf16[32,1,16,64]{3,2,1,0:T(8,128)(2,1)S(1)} %collective-permute-done.1) | copy-start | bytes 196612
  276.8 6.8 %collective-permute-start.2 = (bf16[32,1,16,64]{3,2,1,0:T(8,128)(2,1)S(1)}, bf16[32,1,16,64]{3,2,1,0:T(8,128)(2,1)S(1)}, u32[]{:S(2)}, u32[]{:S(2)}) collective-permute-start(bf16[32,1,16,64]{3,2,1,0:T(8,128)(2,1)S(1)} %get-tuple-element.75), channel_id=1, source_target_pairs={{0,1},{1,2},{2,3},{3,4},{4,5},{5,6},{6,7},{7,8},{8,9},{9,10},{10,1... | collective-permute-start | bytes 196616 | tf_op jit(solution)/shard_map/ppermute | solution.py:17
  282.3 3.2 collective-permute-start.3
  292.6 6.1 copy-start.2
  292.6 7.9 %copy-start.12 = (bf16[32,1024]{1,0:T(8,128)(2,1)S(1)}, bf16[32,1024]{1,0:T(8,128)(2,1)}, u32[]{:S(2)}) copy-start(bf16[32,1024]{1,0:T(8,128)(2,1)} %param.5) | copy-start | bytes 196612
  298.7 15.1 %copy-start.8 = (bf16[32,4,1024]{2,1,0:T(4,128)(2,1)S(1)}, bf16[32,4,1024]{2,1,0:T(4,128)(2,1)}, u32[]{:S(2)}) copy-start(bf16[32,4,1024]{2,1,0:T(4,128)(2,1)} %param.7) | copy-start | bytes 786436
  298.7 15.2 %copy-start.9 = (bf16[32,4,1024]{2,1,0:T(4,128)(2,1)S(1)}, bf16[32,4,1024]{2,1,0:T(4,128)(2,1)}, u32[]{:S(2)}) copy-start(bf16[32,4,1024]{2,1,0:T(4,128)(2,1)} %param.4) | copy-start | bytes 786436
  299.8 355.4 %all-gather.5.cloned.1.call-start = ((), (), s32[]{:S(2)}) async-start(), calls=%async_computation.3 | async-start | bytes 8650752 | tf_op jit(solution)/shard_map/all_gather | solution.py:109
  301.6 23.9 %all-to-all-start = ((bf16[32,2,512]{2,1,0:T(2,128)(2,1)}), bf16[32,2,512]{2,1,0:T(2,128)(2,1)}, u32[]{:S(2)}, u32[]{:S(2)}) async-start(bf16[32,2,512]{2,1,0:T(2,128)(2,1)} %reshape.99), calls=%async_computation | async-start | bytes 131072 | tf_op jit(solution)/shard_map/all_to_all | solution.py:106
  313.8 13.8 %copy-start.5 = (bf16[32,1,16,64]{3,2,1,0:T(8,128)(2,1)S(1)}, bf16[32,1,16,64]{3,2,1,0:T(8,128)(2,1)}, u32[]{:S(2)}) copy-start(bf16[32,1,16,64]{3,2,1,0:T(8,128)(2,1)} %copy-done.4) | copy-start | bytes 196612
  313.8 13.8 %copy-start.7 = (bf16[32,1,16,64]{3,2,1,0:T(8,128)(2,1)S(1)}, bf16[32,1,16,64]{3,2,1,0:T(8,128)(2,1)}, u32[]{:S(2)}) copy-start(bf16[32,1,16,64]{3,2,1,0:T(8,128)(2,1)} %copy-done.6) | copy-start | bytes 196612
  327.6 132.7 %copy-start.1 = (f32[32,4,16,64]{3,2,1,0:T(8,128)S(1)}, f32[32,4,16,64]{3,2,1,0:T(8,128)}, u32[]{:S(2)}) copy-start(f32[32,4,16,64]{3,2,1,0:T(8,128)} %get-tuple-element.74) | copy-start | bytes 1572868
  330.6 324.6 %copy-start.3 = (f32[4,8,4,1024]{3,1,2,0:T(8,128)S(1)}, f32[4,8,4,1024]{3,1,2,0:T(8,128)}, u32[]{:S(2)}) copy-start(f32[4,8,4,1024]{3,1,2,0:T(8,128)} %copy.17) | copy-start | bytes 1572868
  330.6 324.6 %copy-start.10 = (bf16[1024,32]{0,1:T(8,128)(2,1)S(1)}, bf16[1024,32]{0,1:T(8,128)(2,1)}, u32[]{:S(2)}) copy-start(bf16[1024,32]{0,1:T(8,128)(2,1)} %all_to_all.17) | copy-start | bytes 196612
Sparse Core Ops, SparseCore 0:
  10.7 242.5 all-gather.2
  299.9 123.4 reduce-scatter.3
  426.2 228.9 all-gather.4
where the time goes:
time: 668 us
  waiting for transfers between devices  447 us (67%)
  blocking collectives  126 us (19%)
  other arithmetic  23.4 us (4%)
  starting transfers between devices  21.7 us (3%)
  local copies, waits for them, and re-layouts  19.8 us (3%)
  matrix products  15.9 us (2%)
  between operations  14 us (2%)
    all_gather x1, waiting for transfers between devices, body(): vol_all = lax.all_gather(flat_vol, 'filter', axis=0, tiled=True)  241 us
    all_gather x1, waiting for transfers between devices, body(): lax.all_gather(mixed_grad, 'filter', axis=0, tiled=True)  191 us
    psum x1, blocking collectives, body(): taps_grad = lax.psum(taps_part, 'space')  126 us
    reduce_sum x2, other arithmetic, tap_grads(): jnp.sum(grad_wide * window.astype(jnp.float32), axis=(1, 2, 3))  14.4 us
  transfers between devices with their start and end apart: 8, of which 5 were waited for; matrix products, arithmetic and copies ran while one was open for 3% of the time, Pallas kernels for 0%

commit v1 on v0

--- a/solution.py
+++ b/solution.py
@@ -106,7 +106,10 @@
     weight_cols = lax.all_to_all(mixing, "filter", split_axis=1, concat_axis=0, tiled=True)
     back_sum = lax.dot_general(
         weight_cols,
-        lax.all_gather(mixed_grad, "filter", axis=0, tiled=True),
+        jnp.concatenate(
+            lax.all_to_all(jnp.stack([mixed_grad] * lax.axis_size("filter")), "filter", 0, 0),
+            axis=0,
+        ),
         (((0,), (0,)), ((), ())),
         preferred_element_type=jnp.float32,
     )

time: 668 us -> 822 us (1.23)
  the two profiles are of different devices: /device:TPU:2 before, /device:TPU:420 now
where the time goes in v1:
time: 822 us; the launch traced here: 821 us
  blocking collectives  445 us (54%)
  waiting for transfers between devices  205 us (25%)
  starting transfers between devices  86.4 us (11%)
  other arithmetic  27.4 us (3%)
  local copies, waits for them, and re-layouts  25.8 us (3%)
  matrix products  16.2 us (2%)
  between operations  15.1 us (2%)
    psum x1, blocking collectives, body(): taps_grad = lax.psum(taps_part, 'space')  445 us
    all_gather x1, waiting for transfers between devices, body(): vol_all = lax.all_gather(flat_vol, 'filter', axis=0, tiled=True)  203 us
    all_to_all x1, starting transfers between devices, body(): lax.all_to_all(mixing, 'filter', split_axis=1, concat_axis=0, tiled=True)  40.6 us
    ppermute x2, starting transfers between devices, padded_2(): after = lax.ppermute(leading, axis, down)  29.1 us
  transfers between devices with their start and end apart: 8, of which 3 were waited for; matrix products, arithmetic and copies ran while one was open for 5% of the time, Pallas kernels for 0%

profile of v1, /device:TPU:420, one launch (start us, length us, event | category | flops | bytes accessed | tf_op | source)
XLA Modules:
  0.0 820.8 jit_solution(9270872690832561117)
XLA Ops:
  7.2 0.0 copy-start.6
  7.2 0.0 all-gather.2.cloned.1.call-start
  7.2 1.7 copy.16
  9.0 0.0 all-gather.2.cloned.1.call-update
  9.0 1.3 reshape.69
  10.2 2.5 slice_reduce_fusion.26
  12.9 0.0 copy-start
  13.0 203.2 %all-gather.2.cloned.1.call-done = bf16[1024,4096]{1,0:T(8,128)(2,1)} async-done(((bf16[32,4096]{1,0:T(8,128)(2,1)}), bf16[1024,4096]{1,0:T(8,128)(2,1)}) %all-gather.2.cloned.1.call-update) | async-done | bytes 8388624 | tf_op jit(solution)/shard_map/all_gather | solution.py:85
  216.2 4.9 convolution_convert_fusion
  221.1 0.5 reshape.64
  221.7 1.9 collective-permute-start
  223.6 14.5 %collective-permute-start.1 = (bf16[32,1,16,64]{3,2,1,0:T(8,128)(2,1)S(1)}, bf16[32,1,16,64]{3,2,1,0:T(8,128)(2,1)S(1)}, u32[]{:S(2)}, u32[]{:S(2)}) collective-permute-start(bf16[32,1,16,64]{3,2,1,0:T(8,128)(2,1)S(1)} %get-tuple-element.78), channel_id=1, source_target_pairs={{1,0},{2,1},{3,2},{4,3},{5,4},{6,5},{7,6},{8,7},{9,8},{10,9},{11,1... | collective-permute-start | bytes 196616 | tf_op jit(solution)/shard_map/ppermute | solution.py:18
  238.1 0.3 slice_reduce_fusion.25
  238.5 0.0 copy-start.45
  238.5 0.3 collective-permute-done
  238.8 1.8 collective-permute-done.1
  240.6 0.8 select_maximum_fusion.2
  241.6 11.5 %fusion.72 = (f32[32]{0:T(128)}, f32[32]{0:T(128)}, f32[32]{0:T(128)}, f32[32]{0:T(128)}, f32[32]{0:T(128)}, /*index=5*/f32[32]{0:T(128)}, f32[32]{0:T(128)}, f3...) fusion(bf16[32,6,18,66]{3,2,1,0:T(8,128)(2,1)S(1)} %select_maxi, ...), kind=kLoop, calls=%fused_computation.138 | loop fusion | flops 16776640 | bytes 8001152 | tf_op jit(solution)/shard_map/reduce_sum | solution.py:67
  253.3 1.9 collective-permute-start.2
  255.2 14.6 %collective-permute-start.3 = (bf16[32,1,16,64]{3,2,1,0:T(8,128)(2,1)S(1)}, bf16[32,1,16,64]{3,2,1,0:T(8,128)(2,1)S(1)}, u32[]{:S(2)}, u32[]{:S(2)}) collective-permute-start(bf16[32,1,16,64]{3,2,1,0:T(8,128)(2,1)S(1)} %get-tuple-element.76), channel_id=1, source_target_pairs={{1,0},{2,1},{3,2},{4,3},{5,4},{6,5},{7,6},{8,7},{9,8},{10,9},{11,1... | collective-permute-start | bytes 196616 | tf_op jit(solution)/shard_map/ppermute | solution.py:18
  269.9 1.0 copy.12
  270.9 0.9 reshape.100
  271.7 40.6 %all-to-all-start.1 = ((bf16[32,2,512]{2,1,0:T(2,128)(2,1)}), bf16[32,2,512]{2,1,0:T(2,128)(2,1)S(1)}, u32[]{:S(2)}, u32[]{:S(2)}) async-start(bf16[32,2,512]{2,1,0:T(2,128)(2,1)} %reshape.100), calls=%async_computation.1 | async-start | bytes 131072 | tf_op jit(solution)/shard_map/all_to_all | solution.py:106
  312.4 0.0 collective-permute-done.3
  312.4 0.8 select_maximum_fusion
  313.3 6.7 fusion.73
  320.0 0.5 stack_reshape.2
  320.5 0.0 copy-start.7
  320.5 4.3 stack.87
  324.8 12.6 %all-to-all-start = ((bf16[32,32,4096]{2,1,0:T(8,128)(2,1)}), bf16[32,32,4096]{2,1,0:T(8,128)(2,1)}, u32[]{:S(2)}, u32[]{:S(2)}) async-start(bf16[32,32,4096]{2,1,0:T(8,128)(2,1)} %stack.87), calls=%async_computation | async-start | bytes 16777216 | tf_op jit(solution)/shard_map/all_to_all | solution.py:110
  337.4 0.2 reduce-scatter.4.cloned.1.call-start
  337.6 1.9 convert_element_type.292
  339.5 2.2 reshape.67
  341.7 2.2 copy.17
  343.9 1.8 reshape.101
  345.7 2.4 add_convert_fusion
  348.1 2.1 reshape.65
  350.3 3.4 fusion.71
  353.9 0.1 stack.115
  354.0 0.0 copy-start.3
  354.0 6.0 convolution_multiply_fusion
  360.0 1.1 copy.14
  361.1 0.0 reduce-scatter.4.cloned.1.call-update
  361.1 444.6 %psum.7 = f32[32,27]{0,1:T(8,128)S(1)} all-reduce(f32[32,27]{0,1:T(8,128)S(1)} %broadcast_multiply_fusion), channel_id=1, replica_groups=mesh['filter'=32,'space'=16] {'space'}, use_global_device_ids=true, to_apply=%region_28.29 | all-reduce | flops 864 | bytes 6912 | tf_op jit(solution)/shard_map/psum | solution.py:105
  805.7 0.7 copy.13
  806.4 1.4 copy.15
  807.8 5.2 fusion.1
  813.1 0.9 reshape.66
  (132 shorter events, 0.3 us)
Async XLA Ops:
  7.2 209.0 %copy-start.6 = (bf16[32,1024]{1,0:T(8,128)(2,1)S(1)}, bf16[32,1024]{1,0:T(8,128)(2,1)}, u32[]{:S(2)}) copy-start(bf16[32,1024]{1,0:T(8,128)(2,1)} %param.5) | copy-start | bytes 196612
  7.2 209.0 %all-gather.2.cloned.1.call-start = ((), (), s32[]{:S(2)}) async-start(), calls=%async_computation.3 | async-start | bytes 8650752 | tf_op jit(solution)/shard_map/all_gather | solution.py:85
  12.8 228.6 %copy-start.8 = (f32[32]{0:T(128)}, f32[32]{0:T(128)S(1)}, u32[]{:S(2)}) copy-start(f32[32]{0:T(128)S(1)} %get-tuple-element.50) | copy-start | bytes 388
  12.8 228.6 %copy-start.10 = (f32[32]{0:T(128)}, f32[32]{0:T(128)S(1)}, u32[]{:S(2)}) copy-start(f32[32]{0:T(128)S(1)} %get-tuple-element.51) | copy-start | bytes 388
  12.8 228.6 %copy-start.12 = (f32[32]{0:T(128)}, f32[32]{0:T(128)S(1)}, u32[]{:S(2)}) copy-start(f32[32]{0:T(128)S(1)} %get-tuple-element.52) | copy-start | bytes 388
  12.8 228.6 %copy-start.14 = (f32[32]{0:T(128)}, f32[32]{0:T(128)S(1)}, u32[]{:S(2)}) copy-start(f32[32]{0:T(128)S(1)} %get-tuple-element.53) | copy-start | bytes 388
  12.8 228.6 %copy-start.16 = (f32[32]{0:T(128)}, f32[32]{0:T(128)S(1)}, u32[]{:S(2)}) copy-start(f32[32]{0:T(128)S(1)} %get-tuple-element.54) | copy-start | bytes 388
  12.8 228.6 %copy-start.18 = (f32[32]{0:T(128)}, f32[32]{0:T(128)S(1)}, u32[]{:S(2)}) copy-start(f32[32]{0:T(128)S(1)} %get-tuple-element.55) | copy-start | bytes 388
  12.9 228.6 %copy-start.20 = (f32[32]{0:T(128)}, f32[32]{0:T(128)S(1)}, u32[]{:S(2)}) copy-start(f32[32]{0:T(128)S(1)} %get-tuple-element.56) | copy-start | bytes 388
  12.9 228.6 %copy-start.22 = (f32[32]{0:T(128)}, f32[32]{0:T(128)S(1)}, u32[]{:S(2)}) copy-start(f32[32]{0:T(128)S(1)} %get-tuple-element.57) | copy-start | bytes 388
  12.9 228.6 %copy-start.24 = (f32[32]{0:T(128)}, f32[32]{0:T(128)S(1)}, u32[]{:S(2)}) copy-start(f32[32]{0:T(128)S(1)} %get-tuple-element.58) | copy-start | bytes 388
  12.9 228.6 %copy-start.26 = (f32[32]{0:T(128)}, f32[32]{0:T(128)S(1)}, u32[]{:S(2)}) copy-start(f32[32]{0:T(128)S(1)} %get-tuple-element.59) | copy-start | bytes 388
  12.9 228.6 %copy-start.28 = (f32[32]{0:T(128)}, f32[32]{0:T(128)S(1)}, u32[]{:S(2)}) copy-start(f32[32]{0:T(128)S(1)} %get-tuple-element.60) | copy-start | bytes 388
  12.9 228.6 %copy-start.30 = (f32[32]{0:T(128)}, f32[32]{0:T(128)S(1)}, u32[]{:S(2)}) copy-start(f32[32]{0:T(128)S(1)} %get-tuple-element.61) | copy-start | bytes 388
  12.9 228.6 %copy-start.32 = (f32[32]{0:T(128)}, f32[32]{0:T(128)S(1)}, u32[]{:S(2)}) copy-start(f32[32]{0:T(128)S(1)} %get-tuple-element.62) | copy-start | bytes 388
  12.9 228.6 %copy-start.34 = (f32[32]{0:T(128)}, f32[32]{0:T(128)S(1)}, u32[]{:S(2)}) copy-start(f32[32]{0:T(128)S(1)} %get-tuple-element.63) | copy-start | bytes 388
  12.9 228.6 %copy-start.36 = (f32[32]{0:T(128)}, f32[32]{0:T(128)S(1)}, u32[]{:S(2)}) copy-start(f32[32]{0:T(128)S(1)} %get-tuple-element.64) | copy-start | bytes 388
  12.9 225.2 %copy-start = (f32[32,27]{1,0:T(8,128)S(1)}, f32[32,27]{1,0:T(8,128)}, u32[]{:S(2)}) copy-start(f32[32,27]{1,0:T(8,128)} %param.6) | copy-start | bytes 10372
  221.7 17.1 %collective-permute-start = (bf16[32,1,16,64]{3,2,1,0:T(8,128)(2,1)S(1)}, bf16[32,1,16,64]{3,2,1,0:T(8,128)(2,1)S(1)}, u32[]{:S(2)}, u32[]{:S(2)}) collective-permute-start(bf16[32,1,16,64]{3,2,1,0:T(8,128)(2,1)S(1)} %get-tuple-element.77), channel_id=1, source_target_pairs={{0,1},{1,2},{2,3},{3,4},{4,5},{5,6},{6,7},{7,8},{8,9},{9,10},{10,1... | collective-permute-start | bytes 196616 | tf_op jit(solution)/shard_map/ppermute | solution.py:17
  223.6 17.0 %collective-permute-start.1 = (bf16[32,1,16,64]{3,2,1,0:T(8,128)(2,1)S(1)}, bf16[32,1,16,64]{3,2,1,0:T(8,128)(2,1)S(1)}, u32[]{:S(2)}, u32[]{:S(2)}) collective-permute-start(bf16[32,1,16,64]{3,2,1,0:T(8,128)(2,1)S(1)} %get-tuple-element.78), channel_id=1, source_target_pairs={{1,0},{2,1},{3,2},{4,3},{5,4},{6,5},{7,6},{8,7},{9,8},{10,9},{11,1... | collective-permute-start | bytes 196616 | tf_op jit(solution)/shard_map/ppermute | solution.py:18
  238.4 14.6 %copy-start.38 = (f32[32]{0:T(128)}, f32[32]{0:T(128)S(1)}, u32[]{:S(2)}) copy-start(f32[32]{0:T(128)S(1)} %get-tuple-element.65) | copy-start | bytes 388
  238.4 14.6 %copy-start.40 = (f32[32]{0:T(128)}, f32[32]{0:T(128)S(1)}, u32[]{:S(2)}) copy-start(f32[32]{0:T(128)S(1)} %get-tuple-element.66) | copy-start | bytes 388
  238.4 14.6 %copy-start.41 = (f32[32]{0:T(128)}, f32[32]{0:T(128)S(1)}, u32[]{:S(2)}) copy-start(f32[32]{0:T(128)S(1)} %get-tuple-element.67) | copy-start | bytes 388
  238.4 14.6 %copy-start.42 = (f32[32]{0:T(128)}, f32[32]{0:T(128)S(1)}, u32[]{:S(2)}) copy-start(f32[32]{0:T(128)S(1)} %get-tuple-element.68) | copy-start | bytes 388
  238.5 14.6 %copy-start.43 = (f32[32]{0:T(128)}, f32[32]{0:T(128)S(1)}, u32[]{:S(2)}) copy-start(f32[32]{0:T(128)S(1)} %get-tuple-element.69) | copy-start | bytes 388
  253.1 60.1 %copy-start.9 = (f32[32]{0:T(128)S(1)}, f32[32]{0:T(128)}, u32[]{:S(2)}) copy-start(f32[32]{0:T(128)} %copy-done.8) | copy-start | bytes 388
  253.1 60.1 %copy-start.11 = (f32[32]{0:T(128)S(1)}, f32[32]{0:T(128)}, u32[]{:S(2)}) copy-start(f32[32]{0:T(128)} %copy-done.10) | copy-start | bytes 388
  253.1 60.1 %copy-start.13 = (f32[32]{0:T(128)S(1)}, f32[32]{0:T(128)}, u32[]{:S(2)}) copy-start(f32[32]{0:T(128)} %copy-done.12) | copy-start | bytes 388
  253.2 60.1 %copy-start.15 = (f32[32]{0:T(128)S(1)}, f32[32]{0:T(128)}, u32[]{:S(2)}) copy-start(f32[32]{0:T(128)} %copy-done.14) | copy-start | bytes 388
  253.2 60.1 %copy-start.17 = (f32[32]{0:T(128)S(1)}, f32[32]{0:T(128)}, u32[]{:S(2)}) copy-start(f32[32]{0:T(128)} %copy-done.16) | copy-start | bytes 388
  253.2 60.1 %copy-start.19 = (f32[32]{0:T(128)S(1)}, f32[32]{0:T(128)}, u32[]{:S(2)}) copy-start(f32[32]{0:T(128)} %copy-done.18) | copy-start | bytes 388
  253.2 60.1 %copy-start.21 = (f32[32]{0:T(128)S(1)}, f32[32]{0:T(128)}, u32[]{:S(2)}) copy-start(f32[32]{0:T(128)} %copy-done.20) | copy-start | bytes 388
  253.2 60.1 %copy-start.23 = (f32[32]{0:T(128)S(1)}, f32[32]{0:T(128)}, u32[]{:S(2)}) copy-start(f32[32]{0:T(128)} %copy-done.22) | copy-start | bytes 388
  253.2 60.1 %copy-start.25 = (f32[32]{0:T(128)S(1)}, f32[32]{0:T(128)}, u32[]{:S(2)}) copy-start(f32[32]{0:T(128)} %copy-done.24) | copy-start | bytes 388
  253.2 60.1 %copy-start.27 = (f32[32]{0:T(128)S(1)}, f32[32]{0:T(128)}, u32[]{:S(2)}) copy-start(f32[32]{0:T(128)} %copy-done.26) | copy-start | bytes 388
  253.2 60.1 %copy-start.29 = (f32[32]{0:T(128)S(1)}, f32[32]{0:T(128)}, u32[]{:S(2)}) copy-start(f32[32]{0:T(128)} %copy-done.28) | copy-start | bytes 388
  253.2 60.1 %copy-start.31 = (f32[32]{0:T(128)S(1)}, f32[32]{0:T(128)}, u32[]{:S(2)}) copy-start(f32[32]{0:T(128)} %copy-done.30) | copy-start | bytes 388
  253.2 60.1 %copy-start.33 = (f32[32]{0:T(128)S(1)}, f32[32]{0:T(128)}, u32[]{:S(2)}) copy-start(f32[32]{0:T(128)} %copy-done.32) | copy-start | bytes 388
  253.3 60.1 %copy-start.35 = (f32[32]{0:T(128)S(1)}, f32[32]{0:T(128)}, u32[]{:S(2)}) copy-start(f32[32]{0:T(128)} %copy-done.34) | copy-start | bytes 388
  253.3 60.1 %copy-start.37 = (f32[32]{0:T(128)S(1)}, f32[32]{0:T(128)}, u32[]{:S(2)}) copy-start(f32[32]{0:T(128)} %copy-done.36) | copy-start | bytes 388
  253.3 60.1 %copy-start.39 = (f32[32]{0:T(128)S(1)}, f32[32]{0:T(128)}, u32[]{:S(2)}) copy-start(f32[32]{0:T(128)} %copy-done.38) | copy-start | bytes 388
  253.3 59.0 %collective-permute-start.2 = (bf16[32,1,16,64]{3,2,1,0:T(8,128)(2,1)S(1)}, bf16[32,1,16,64]{3,2,1,0:T(8,128)(2,1)S(1)}, u32[]{:S(2)}, u32[]{:S(2)}) collective-permute-start(bf16[32,1,16,64]{3,2,1,0:T(8,128)(2,1)S(1)} %get-tuple-element.75), channel_id=1, source_target_pairs={{0,1},{1,2},{2,3},{3,4},{4,5},{5,6},{6,7},{7,8},{8,9},{9,10},{10,1... | collective-permute-start | bytes 196616 | tf_op jit(solution)/shard_map/ppermute | solution.py:17
  255.2 57.1 %collective-permute-start.3 = (bf16[32,1,16,64]{3,2,1,0:T(8,128)(2,1)S(1)}, bf16[32,1,16,64]{3,2,1,0:T(8,128)(2,1)S(1)}, u32[]{:S(2)}, u32[]{:S(2)}) collective-permute-start(bf16[32,1,16,64]{3,2,1,0:T(8,128)(2,1)S(1)} %get-tuple-element.76), channel_id=1, source_target_pairs={{1,0},{2,1},{3,2},{4,3},{5,4},{6,5},{7,6},{8,7},{9,8},{10,9},{11,1... | collective-permute-start | bytes 196616 | tf_op jit(solution)/shard_map/ppermute | solution.py:18
  271.7 48.7 %all-to-all-start.1 = ((bf16[32,2,512]{2,1,0:T(2,128)(2,1)}), bf16[32,2,512]{2,1,0:T(2,128)(2,1)S(1)}, u32[]{:S(2)}, u32[]{:S(2)}) async-start(bf16[32,2,512]{2,1,0:T(2,128)(2,1)} %reshape.100), calls=%async_computation.1 | async-start | bytes 131072 | tf_op jit(solution)/shard_map/all_to_all | solution.py:106
  324.8 483.1 %all-to-all-start = ((bf16[32,32,4096]{2,1,0:T(8,128)(2,1)}), bf16[32,32,4096]{2,1,0:T(8,128)(2,1)}, u32[]{:S(2)}, u32[]{:S(2)}) async-start(bf16[32,32,4096]{2,1,0:T(8,128)(2,1)} %stack.87), calls=%async_computation | async-start | bytes 16777216 | tf_op jit(solution)/shard_map/all_to_all | solution.py:110
  337.4 469.0 %reduce-scatter.4.cloned.1.call-start = ((), (), s32[]{:S(2)}) async-start(), calls=%async_computation.4 | async-start | bytes 557056
  354.0 453.9 %copy-start.2 = (f32[4,8,4,1024]{3,1,2,0:T(8,128)S(1)}, f32[4,8,4,1024]{3,1,2,0:T(8,128)}, u32[]{:S(2)}) copy-start(f32[4,8,4,1024]{3,1,2,0:T(8,128)} %copy.17) | copy-start | bytes 1572868
  354.0 453.9 %copy-start.3 = (bf16[32,32,32]{2,1,0:T(8,128)(2,1)S(1)}, bf16[32,32,32]{2,1,0:T(8,128)(2,1)}, u32[]{:S(2)}) copy-start(bf16[32,32,32]{2,1,0:T(8,128)(2,1)} %reshape.101) | copy-start | bytes 196612
  (25 other events, 147.6 us)
Sparse Core Ops, SparseCore 0:
  10.7 205.4 all-gather.1
  361.2 165.3 reduce-scatter.3
